TPU v7x, 32 devices: a whole 2x2x4 slice. The times are simulated.
32 devices in a mesh: dp: 8 (over z, x), tensor: 4 (over y, core).
Axes of the slice: x: 2, y: 2, z: 4, core: 2. Of those that a mesh axis runs over, the one named last changes fastest.
Arguments:
- embedded: bfloat16 [8192, 768], P(('dp', 'tensor')), may hold values from -6 to 6
- bigram_ids: int32 [8192], P(('dp', 'tensor')), may hold values from 0 to 16383, as said below
- trigram_ids: int32 [8192], P(('dp', 'tensor')), may hold values from 0 to 16383, as said below
- prefix_lens: int32 [8], P('dp'), may hold values from 102 to 512
- bigram_table: bfloat16 [16384, 192], P('dp'), may hold values from -6 to 6
- trigram_table: bfloat16 [16384, 192], P('dp'), may hold values from -6 to 6
- ngram_weight: bfloat16 [384, 768], replicated, may hold values from -0.3125 to 0.3125
- first_gain: float32 [768], replicated, may hold values from 0.5 to 1.5
- attend_weight: bfloat16 [768, 2304], P(None, 'tensor'), may hold values from -0.21875 to 0.21875
- output_weight: bfloat16 [768, 768], P('tensor'), may hold values from -0.875 to 0.875
- second_gain: float32 [768], replicated, may hold values from 0.5 to 1.5
- gate_weight: bfloat16 [768, 2048], P(None, 'tensor'), may hold values from -0.21875 to 0.21875
- up_weight: bfloat16 [768, 2048], P(None, 'tensor'), may hold values from -0.21875 to 0.21875
- down_weight: bfloat16 [2048, 768], P('tensor'), may hold values from -0.125 to 0.125
- cotangent: bfloat16 [8192, 768], P('dp'), may hold values from -6 to 6
Outputs:
- block_out: bfloat16 [8192, 768], P(('dp', 'tensor'))
- embed_grad: float32 [8192, 768], P(('dp', 'tensor'))
- bigram_grad: float32 [16384, 192], P(('dp', 'tensor'))
- trigram_grad: float32 [16384, 192], P(('dp', 'tensor'))
- ngram_weight_grad: float32 [384, 768], P(None, ('dp', 'tensor'))
- first_gain_grad: float32 [768], P(('dp', 'tensor'))
- attend_weight_grad: float32 [768, 2304], P('dp', 'tensor')
- output_weight_grad: float32 [768, 768], P('tensor', 'dp')
- second_gain_grad: float32 [768], P(('dp', 'tensor'))
- gate_weight_grad: float32 [768, 2048], P('dp', 'tensor')
- up_weight_grad: float32 [768, 2048], P('dp', 'tensor')
- down_weight_grad: float32 [2048, 768], P('tensor', 'dp')
Inputs may be any that keep to these rules, and one draw needn't show every extreme that they name: `bigram_ids`: row r of the 2-gram table is held by index r // 2048 of dp. Among the tokens of one device, at most 64 name rows of one holder; in every draw one holder gets exactly 64 from every device. `trigram_ids`: row r of the 3-gram table is held by index r // 2048 of dp. Among the tokens of one device, at most 64 name rows of one holder; in every draw one holder gets exactly 64 from every device.
All inputs are finite; a program needn't handle non-finite values.
Results may differ from a plain program's by a relative error of at most 0.022.
Values may be sent and summed in bfloat16 or wider, within the bound.
A program may use at most 128 MiB of HBM per device.

v0:
```python
import math
import jax
import jax.numpy as jnp
from jax import lax
from jax.sharding import PartitionSpec as P

HD = 64


def normed_rows(values_in, gain):
    scaling = lax.rsqrt(jnp.mean(values_in * values_in, axis=-1, keepdims=True) + 1e-05)
    return (values_in * scaling * gain, scaling)


def norm_backward(grad_out, values_in, scaling, gain):
    scaled = grad_out * gain
    gain_grad = jnp.sum(grad_out * values_in * scaling, axis=0)
    row_grad = scaling * scaled - values_in * scaling**3 * jnp.mean(
        scaled * values_in, axis=-1, keepdims=True
    )
    return (row_grad, gain_grad)


def rotary_tables(length, width):
    halfway = width // 2
    frequency = jnp.exp(jnp.arange(halfway, dtype=jnp.float32) * (-2.0 * math.log(10000.0) / width))
    angles = jnp.arange(length, dtype=jnp.float32)[:, None] * frequency[None, :]
    return (jnp.cos(angles), jnp.sin(angles))


def rotate(values_in, cosine, sines):
    halfway = values_in.shape[-1] // 2
    leading = values_in[..., :halfway]
    trailing = values_in[..., halfway:]
    cosine = cosine[:, None, :]
    sines = sines[:, None, :]
    return jnp.concatenate(
        [leading * cosine - trailing * sines, trailing * cosine + leading * sines], axis=-1
    )


def unrotate(grads, cosine, sines):
    halfway = grads.shape[-1] // 2
    leading = grads[..., :halfway]
    trailing = grads[..., halfway:]
    cosine = cosine[:, None, :]
    sines = sines[:, None, :]
    return jnp.concatenate(
        [leading * cosine + trailing * sines, trailing * cosine - leading * sines], axis=-1
    )


def inner(left, right):
    return lax.dot_general(
        left, right, (((0,), (0,)), ((), ())), preferred_element_type=jnp.float32
    )


def slot_positions(row_ids, rows_dev, peer_count, capacity):
    owner = row_ids // rows_dev
    onehot = (owner[:, None] == jnp.arange(peer_count)[None, :]).astype(jnp.float32)
    tokens = row_ids.shape[0]
    earlier = (jnp.arange(tokens)[None, :] < jnp.arange(tokens)[:, None]).astype(jnp.float32)
    ranks = jnp.dot(earlier, onehot, precision=lax.Precision.HIGHEST)
    slot = jnp.sum(ranks * onehot, axis=1).astype(jnp.int32)
    return owner * capacity + slot


def shards(
    embedded,
    bigram_ids,
    trigram_ids,
    prefix_lens,
    bigram_table,
    trigram_table,
    ngram_weight,
    first_gain,
    attend_weight,
    output_weight,
    second_gain,
    gate_weight,
    up_weight,
    down_weight,
    cotangent,
):
    peer_count = lax.axis_size("dp")
    split_count = lax.axis_size("tensor")
    local_rows = embedded.shape[0]
    length = local_rows * split_count
    rows_dev = bigram_table.shape[0]
    table_width = bigram_table.shape[1]
    capacity = max(4, 2 * local_rows // peer_count)
    scaling_factor = HD ** (-0.5)
    bigram_slot = slot_positions(bigram_ids, rows_dev, peer_count, capacity)
    trigram_slot = slot_positions(trigram_ids, rows_dev, peer_count, capacity)
    requests = jnp.zeros((2, peer_count * capacity), jnp.int32)
    requests = requests.at[0, bigram_slot].set(bigram_ids % rows_dev + 1)
    requests = requests.at[1, trigram_slot].set(trigram_ids % rows_dev + 1)
    requests = requests.reshape(2, peer_count, capacity)
    asked_rows = lax.all_to_all(requests, "dp", split_axis=1, concat_axis=1, tiled=True)
    picked = jnp.maximum(asked_rows - 1, 0)
    found_rows = jnp.stack([bigram_table[picked[0]], trigram_table[picked[1]]])
    answer = lax.all_to_all(found_rows, "dp", split_axis=1, concat_axis=1, tiled=True)
    fetched, asked_rows = (answer, asked_rows)
    fetched = fetched.reshape(2, peer_count * capacity, table_width)
    ngram_rows = jnp.concatenate([fetched[0][bigram_slot], fetched[1][trigram_slot]], axis=1)
    lifted = jnp.dot(ngram_rows, ngram_weight, preferred_element_type=jnp.float32)
    inputs = embedded.astype(jnp.float32) + lifted
    normed_one, first_scale = normed_rows(inputs, first_gain)
    normed_one_full = lax.all_gather(normed_one.astype(jnp.bfloat16), "tensor", axis=0, tiled=True)
    head_count = attend_weight.shape[1] // (3 * HD)
    mixture = jnp.dot(normed_one_full, attend_weight, preferred_element_type=jnp.float32)
    mixture = mixture.reshape(length, head_count, 3, HD)
    cosine, sines = rotary_tables(length, HD)
    queries = rotate(mixture[:, :, 0], cosine, sines).astype(jnp.bfloat16)
    keys = rotate(mixture[:, :, 1], cosine, sines).astype(jnp.bfloat16)
    values = mixture[:, :, 2].astype(jnp.bfloat16)
    block_size = min(512, length)
    block_count = length // block_size
    prefix = prefix_lens[0]
    key_position = jnp.arange(length)

    def scores_of(query_block, offset):
        products = (
            jnp.einsum("qhd,khd->hqk", query_block, keys, preferred_element_type=jnp.float32)
            * scaling_factor
        )
        query_position = offset + jnp.arange(block_size)
        allowed = (key_position[None, :] <= query_position[:, None]) | (
            key_position[None, :] < prefix
        )
        return jnp.where(allowed[None], products, -1000000000.0)

    def forward_block(position):
        offset = position * block_size
        query_block = lax.dynamic_slice_in_dim(queries, offset, block_size, 0)
        scores = scores_of(query_block, offset)
        highest_score = jnp.max(scores, axis=-1, keepdims=True)
        powers = jnp.exp(scores - highest_score)
        totals = jnp.sum(powers, axis=-1, keepdims=True)
        weights_low = (powers / totals).astype(jnp.bfloat16)
        result = jnp.einsum("hqk,khd->qhd", weights_low, values, preferred_element_type=jnp.float32)
        return (result.astype(jnp.bfloat16), (highest_score + jnp.log(totals))[..., 0])

    attended, log_totals = lax.map(forward_block, jnp.arange(block_count))
    attended = attended.reshape(length, head_count * HD)
    part_rows = attended
    branch_one = lax.psum_scatter(
        jnp.dot(part_rows, output_weight, preferred_element_type=jnp.float32).astype(jnp.bfloat16),
        "tensor",
        scatter_dimension=0,
        tiled=True,
    ).astype(jnp.float32)
    after = inputs + branch_one
    normed_two, second_scale = normed_rows(after, second_gain)
    normed_two_full = lax.all_gather(normed_two.astype(jnp.bfloat16), "tensor", axis=0, tiled=True)
    gate = jnp.dot(normed_two_full, gate_weight, preferred_element_type=jnp.float32)
    up_part = jnp.dot(normed_two_full, up_weight, preferred_element_type=jnp.float32)
    sigmoid_gate = jax.nn.sigmoid(gate)
    activity = (gate * sigmoid_gate * up_part).astype(jnp.bfloat16)
    part_rows = activity
    branch_two = lax.psum_scatter(
        jnp.dot(part_rows, down_weight, preferred_element_type=jnp.float32).astype(jnp.bfloat16),
        "tensor",
        scatter_dimension=0,
        tiled=True,
    ).astype(jnp.float32)
    block_out = (after + branch_two).astype(jnp.bfloat16)
    own_cot = lax.dynamic_slice_in_dim(
        cotangent, lax.axis_index("tensor") * local_rows, local_rows, 0
    ).astype(jnp.float32)
    down_grad = inner(activity, cotangent)
    activity_back = jnp.dot(cotangent, down_weight.T, preferred_element_type=jnp.float32)
    gate_back = (
        activity_back * up_part * sigmoid_gate * (1.0 + gate * (1.0 - sigmoid_gate))
    ).astype(jnp.bfloat16)
    up_back = (activity_back * gate * sigmoid_gate).astype(jnp.bfloat16)
    gate_grad = inner(normed_two_full, gate_back)
    up_grad = inner(normed_two_full, up_back)
    normed_two_back = lax.psum_scatter(
        (
            jnp.dot(gate_back, gate_weight.T, preferred_element_type=jnp.float32)
            + jnp.dot(up_back, up_weight.T, preferred_element_type=jnp.float32)
        ).astype(jnp.bfloat16),
        "tensor",
        scatter_dimension=0,
        tiled=True,
    ).astype(jnp.float32)
    second_row_grad, second_partial = norm_backward(
        normed_two_back, after, second_scale, second_gain
    )
    after_grad = own_cot + second_row_grad
    attn_back_full = lax.all_gather(after_grad.astype(jnp.bfloat16), "tensor", axis=0, tiled=True)
    output_grad = inner(attended, attn_back_full)
    attended_back = jnp.dot(
        attn_back_full, output_weight.T, preferred_element_type=jnp.float32
    ).astype(jnp.bfloat16)
    attended_back = attended_back.reshape(length, head_count, HD)

    def backward_block(carry, item):
        key_sum, value_sum = carry
        position, log_block = item
        offset = position * block_size
        query_block = lax.dynamic_slice_in_dim(queries, offset, block_size, 0)
        grad_block = lax.dynamic_slice_in_dim(attended_back, offset, block_size, 0)
        probs = jnp.exp(scores_of(query_block, offset) - log_block[..., None])
        prob_back = jnp.einsum(
            "qhd,khd->hqk", grad_block, values, preferred_element_type=jnp.float32
        )
        centre = jnp.sum(probs * prob_back, axis=-1, keepdims=True)
        score_back = (probs * (prob_back - centre)).astype(jnp.bfloat16)
        query_grad = (
            jnp.einsum("hqk,khd->qhd", score_back, keys, preferred_element_type=jnp.float32)
            * scaling_factor
        )
        key_sum = (
            key_sum
            + jnp.einsum(
                "hqk,qhd->khd", score_back, query_block, preferred_element_type=jnp.float32
            )
            * scaling_factor
        )
        value_sum = value_sum + jnp.einsum(
            "hqk,qhd->khd",
            probs.astype(jnp.bfloat16),
            grad_block,
            preferred_element_type=jnp.float32,
        )
        return ((key_sum, value_sum), query_grad)

    zero_heads = jnp.zeros((length, head_count, HD), jnp.float32)
    (key_sum, value_sum), query_grads = lax.scan(
        backward_block, (zero_heads, zero_heads), (jnp.arange(block_count), log_totals)
    )
    query_back = (
        query_grads.reshape(length, head_count, HD).astype(jnp.bfloat16).astype(jnp.float32)
    )
    key_back = key_sum.astype(jnp.bfloat16).astype(jnp.float32)
    mixture_back = jnp.stack(
        [unrotate(query_back, cosine, sines), unrotate(key_back, cosine, sines), value_sum], axis=2
    )
    mixture_back = mixture_back.reshape(length, head_count * 3 * HD).astype(jnp.bfloat16)
    attend_grad = inner(normed_one_full, mixture_back)
    part_rows = mixture_back
    normed_one_back = lax.psum_scatter(
        jnp.dot(part_rows, attend_weight.T, preferred_element_type=jnp.float32).astype(
            jnp.bfloat16
        ),
        "tensor",
        scatter_dimension=0,
        tiled=True,
    ).astype(jnp.float32)
    first_row_grad, first_partial = norm_backward(normed_one_back, inputs, first_scale, first_gain)
    embed_grad = after_grad + first_row_grad
    lifted_back = embed_grad.astype(jnp.bfloat16)
    ngram_partial = inner(ngram_rows, lifted_back)
    row_back = jnp.dot(lifted_back, ngram_weight.T, preferred_element_type=jnp.float32)
    outgoing = jnp.zeros((2, peer_count * capacity, table_width), jnp.float32)
    outgoing = outgoing.at[0, bigram_slot].set(row_back[:, :table_width])
    outgoing = outgoing.at[1, trigram_slot].set(row_back[:, table_width:])
    outgoing = outgoing.reshape(2, peer_count, capacity, table_width)
    arrived = lax.all_to_all(
        outgoing.astype(jnp.bfloat16), "dp", split_axis=1, concat_axis=1, tiled=True
    ).astype(outgoing.dtype)
    picked_rows = jnp.maximum(asked_rows - 1, 0)
    bigram_part = (
        jnp.zeros((rows_dev, table_width), jnp.float32)
        .at[picked_rows[0].reshape(-1)]
        .add(arrived[0].reshape(-1, table_width))
    )
    trigram_part = (
        jnp.zeros((rows_dev, table_width), jnp.float32)
        .at[picked_rows[1].reshape(-1)]
        .add(arrived[1].reshape(-1, table_width))
    )
    attend_sum, output_sum, gate_sum, up_sum, down_sum, ngram_group, first_group, second_group = (
        lax.psum_scatter(attend_grad, "dp", scatter_dimension=0, tiled=True),
        lax.psum_scatter(output_grad, "dp", scatter_dimension=1, tiled=True),
        lax.psum_scatter(gate_grad, "dp", scatter_dimension=0, tiled=True),
        lax.psum_scatter(up_grad, "dp", scatter_dimension=0, tiled=True),
        lax.psum_scatter(down_grad, "dp", scatter_dimension=1, tiled=True),
        lax.psum_scatter(ngram_partial, "dp", scatter_dimension=1, tiled=True),
        lax.psum_scatter(first_partial, "dp", scatter_dimension=0, tiled=True),
        lax.psum_scatter(second_partial, "dp", scatter_dimension=0, tiled=True),
    )
    bigram_grad, trigram_grad, ngram_grad, first_grad, second_grad = (
        lax.psum_scatter(
            bigram_part.astype(jnp.bfloat16), "tensor", scatter_dimension=0, tiled=True
        ).astype(jnp.float32),
        lax.psum_scatter(
            trigram_part.astype(jnp.bfloat16), "tensor", scatter_dimension=0, tiled=True
        ).astype(jnp.float32),
        lax.psum_scatter(
            ngram_group.astype(jnp.bfloat16), "tensor", scatter_dimension=1, tiled=True
        ).astype(jnp.float32),
        lax.psum_scatter(
            first_group.astype(jnp.bfloat16), "tensor", scatter_dimension=0, tiled=True
        ).astype(jnp.float32),
        lax.psum_scatter(
            second_group.astype(jnp.bfloat16), "tensor", scatter_dimension=0, tiled=True
        ).astype(jnp.float32),
    )
    return (
        block_out,
        embed_grad,
        bigram_grad,
        trigram_grad,
        ngram_grad,
        first_grad,
        attend_sum,
        output_sum,
        second_grad,
        gate_sum,
        up_sum,
        down_sum,
    )


def solution(mesh):
    placed = (
        P(("dp", "tensor"), None),
        P(("dp", "tensor")),
        P(("dp", "tensor")),
        P("dp"),
        P("dp", None),
        P("dp", None),
        P(),
        P(),
        P(None, "tensor"),
        P("tensor", None),
        P(),
        P(None, "tensor"),
        P(None, "tensor"),
        P("tensor", None),
        P("dp", None),
    )
    return jax.shard_map(
        shards,
        mesh=mesh,
        in_specs=placed,
        out_specs=(
            P(("dp", "tensor"), None),
            P(("dp", "tensor"), None),
            P(("dp", "tensor"), None),
            P(("dp", "tensor"), None),
            P(None, ("dp", "tensor")),
            P(("dp", "tensor")),
            P("dp", "tensor"),
            P("tensor", "dp"),
            P(("dp", "tensor")),
            P("dp", "tensor"),
            P("dp", "tensor"),
            P("tensor", "dp"),
        ),
        check_vma=False,
    )
```

profile of v0, /device:TPU:0, one launch (start us, length us, event | category | flops | bytes accessed | tf_op | source)
XLA Modules:
  0.0 817.6 jit_solution(4274439268550508631)
XLA Ops:
  9.2 12.4 %scatter_fusion = s32[2,512]{1,0:T(2,128)S(1)} fusion(s32[2,512]{1,0:T(2,128)S(1)} %broadcast_in_dim.44, s32[256]{0:T(256)S(1)} %bitcast.157, s32[256]{0:T(256)S(1)} %get-tuple-element.362), kind=kCustom, calls=%fused_computation.4 | custom fusion | bytes 5120 | tf_op jit(solution)/shard_map/scatter | solution.py:97
  21.6 12.4 %scatter_fusion.1 = s32[2,512]{1,0:T(2,128)S(1)} fusion(s32[2,512]{1,0:T(2,128)S(1)} %scatter_fusion, s32[256]{0:T(256)S(1)} %bitcast.159, s32[256]{0:T(256)S(1)} %get-tuple-element.360), kind=kCustom, calls=%fused_computation.5 | custom fusion | bytes 5120 | tf_op jit(solution)/shard_map/scatter | solution.py:98
  34.7 7.3 all-to-all-start
  44.0 4.4 all-to-all-done
  58.9 13.2 %all-to-all-done.1 = bf16[2,8,64,192]{3,2,0,1:T(8,128)(2,1)S(1)} async-done(((bf16[2,8,64,192]{3,2,0,1:T(8,128)(2,1)}), bf16[2,8,64,192]{3,2,0,1:T(8,128)(2,1)S(1)}, u32[]{:S(2)}, u32[]{:S(2)}) %all-to-all-start.1) | async-done | bytes 393248 | tf_op jit(solution)/shard_map/all_to_all | solution.py:103
  77.7 17.7 %all-gather.4.cloned.1.call-done = bf16[1024,768]{1,0:T(8,128)(2,1)} async-done(((bf16[256,768]{1,0:T(8,128)(2,1)}), bf16[1024,768]{1,0:T(8,128)(2,1)}) %all-gather.4.cloned.1.call-update) | async-done | bytes 1572880 | tf_op jit(solution)/shard_map/all_gather | solution.py:110
  98.7 15.5 %while.30 = (s32[]{:T(128)}, bf16[2,512,3,64]{1,3,2,0:T(8,128)(2,1)S(1)}, f32[2,3,512]{2,1,0:T(4,128)S(1)}, s32[2]{0:T(128)S(1)}, s32[]{:T(128)}, /*index=5*/bf1...) while((s32[]{:T(128)}, ...), condition=%wide.region_8.9_spmd.clone.clone, body=%wide.region_5.8_spmd.clone.clone.sunk | while | flops 422674432 | bytes 22216908 | solution.py:145
  118.4 28.3 %reduce-scatter.18.cloned.1.call-done = bf16[256,768]{1,0:T(8,128)(2,1)} async-done(((bf16[1024,768]{1,0:T(8,128)(2,1)}), bf16[256,768]{1,0:T(8,128)(2,1)}) %reduce-scatter.18.cloned.1.call-update) | async-done | bytes 393232 | tf_op jit(solution)/shard_map/reduce_scatter | solution.py:148
  150.4 19.8 %all-gather.6.cloned.1.call-done = bf16[1024,768]{1,0:T(8,128)(2,1)} async-done(((bf16[256,768]{1,0:T(8,128)(2,1)}), bf16[1024,768]{1,0:T(8,128)(2,1)}) %all-gather.6.cloned.1.call-update) | async-done | bytes 1572880 | tf_op jit(solution)/shard_map/all_gather | solution.py:156
  181.3 28.3 %reduce-scatter.22.cloned.1.call-done = bf16[256,768]{1,0:T(8,128)(2,1)} async-done(((bf16[1024,768]{1,0:T(8,128)(2,1)}), bf16[256,768]{1,0:T(8,128)(2,1)}) %reduce-scatter.22.cloned.1.call-update) | async-done | bytes 393232 | tf_op jit(solution)/shard_map/reduce_scatter | solution.py:180
  213.9 19.6 %all-gather.8.cloned.1.call-done = bf16[1024,768]{1,0:T(8,128)(2,1)} async-done(((bf16[256,768]{1,0:T(8,128)(2,1)}), bf16[1024,768]{1,0:T(8,128)(2,1)}) %all-gather.8.cloned.1.call-update) | async-done | bytes 1572880 | tf_op jit(solution)/shard_map/all_gather | solution.py:193
  236.3 23.7 %while.31 = (s32[]{:T(128)}, f32[1024,3,64]{0,2,1:T(8,128)S(1)}, f32[1024,3,64]{0,2,1:T(8,128)}, bf16[2,512,3,64]{1,3,2,0:T(8,128)(2,1)}, s32[2]{0:T(128)S(1)}, ...) while((s32[]{:T(128)}, f32[1024,3,64]{0,2,1:T(8,128)S(1)}, ...), condition=%wide.region_16.17_spmd.clone.clone, body=%wide.region_14.16_spmd.clone.clone.sunk | while | flops 1032355840 | bytes 67424672 | solution.py:232
  269.0 25.8 %reduce-scatter.24.cloned.1.call-done = bf16[256,768]{1,0:T(8,128)(2,1)} async-done(((bf16[1024,768]{1,0:T(8,128)(2,1)}), bf16[256,768]{1,0:T(8,128)(2,1)}) %reduce-scatter.24.cloned.1.call-update) | async-done | bytes 393232 | tf_op jit(solution)/shard_map/reduce_scatter | solution.py:245
  296.0 29.6 %reduce-scatter.20.cloned.1.call-done = bf16[256,768]{1,0:T(8,128)(2,1)} async-done(((bf16[1024,768]{1,0:T(8,128)(2,1)}), bf16[256,768]{1,0:T(8,128)(2,1)}) %reduce-scatter.20.cloned.1.call-update) | async-done | bytes 393232 | tf_op jit(solution)/shard_map/reduce_scatter | solution.py:162
  333.6 13.1 %scatter_fusion.2 = f32[2,512,192]{2,1,0:T(8,128)S(1)} fusion(f32[2,512,192]{2,1,0:T(8,128)S(1)} %broadcast_in_dim.58, s32[256]{0:T(256)S(1)} %bitcast.158, f32[256,192]{1,0:T(8,128)S(1)} %get-tuple-element.347), kind=kCustom, calls=%fused_computation.6 | custom fusion | bytes 591872 | tf_op jit(solution)/shard_map/scatter | solution.py:259
  346.7 13.1 %scatter_fusion.3 = f32[2,512,192]{2,1,0:T(8,128)S(1)} fusion(f32[2,512,192]{2,1,0:T(8,128)S(1)} %scatter_fusion.2, s32[256]{0:T(256)S(1)} %bitcast.160, f32[256,192]{1,0:T(8,128)S(1)} %get-tuple-element.346), kind=kCustom, calls=%fused_computation.7 | custom fusion | bytes 591872 | tf_op jit(solution)/shard_map/scatter | solution.py:260
  360.8 5.5 all-to-all-start.2
  366.4 14.4 %all-to-all-done.2 = bf16[2,8,64,192]{3,2,0,1:T(8,128)(2,1)S(1)} async-done(((bf16[2,8,64,192]{3,2,0,1:T(8,128)(2,1)}), bf16[2,8,64,192]{3,2,0,1:T(8,128)(2,1)S(1)}, u32[]{:S(2)}, u32[]{:S(2)}) %all-to-all-start.2) | async-done | bytes 393248 | tf_op jit(solution)/shard_map/all_to_all | solution.py:262
  381.7 4.6 scatter_custom_fusion.4
  387.5 4.1 scatter_custom_fusion.5
  397.5 4.1 fusion.89
  404.2 4.1 fusion.91
  408.4 4.1 fusion.88
  415.0 45.6 %reduce-scatter.40.cloned.1.call-done = f32[96,192]{1,0:T(8,128)} async-done(((f32[768,192]{1,0:T(8,128)}), f32[96,192]{1,0:T(8,128)}) %reduce-scatter.40.cloned.1.call-update) | async-done | bytes 73744
  462.2 19.6 %all-reduce.7 = (bf16[768]{0:T(1024)(128)(2,1)S(1)}, bf16[768]{0:T(1024)(128)(2,1)S(1)}) all-reduce(f32[768]{0:T(1024)S(1)} %get-tuple-element.279, f32[768]{0:T(1024)S(1)} %copy-done.50), channel_id=10, replica_groups=mesh['dp'=8,'tensor'=4] {'dp'}, use_global_device_ids=true, to_apply=%region_28.29.clone | all-reduce | flops 1536 | bytes 9216
  482.0 5.6 all-reduce.8
  490.6 24.0 %reduce-scatter.28.cloned.1.call-done = bf16[512,192]{1,0:T(8,128)(2,1)} async-done(((bf16[2048,192]{1,0:T(8,128)(2,1)}), bf16[512,192]{1,0:T(8,128)(2,1)}) %reduce-scatter.28.cloned.1.call-update) | async-done | bytes 196624 | tf_op jit(solution)/shard_map/reduce_scatter | solution.py:290
  516.5 19.7 %reduce-scatter.42.cloned.1.call-done = bf16[384,24]{0,1:T(8,128)(2,1)} async-done(((bf16[384,96]{0,1:T(8,128)(2,1)}), bf16[384,24]{0,1:T(8,128)(2,1)}) %reduce-scatter.42.cloned.1.call-update) | async-done | bytes 18448
  537.5 67.9 %reduce-scatter.34.cloned.1.call-done = f32[96,512]{1,0:T(8,128)} async-done(((f32[768,512]{1,0:T(8,128)}), f32[96,512]{1,0:T(8,128)}) %reduce-scatter.34.cloned.1.call-update) | async-done | bytes 196624 | tf_op jit(solution)/shard_map/reduce_scatter | solution.py:279
  605.4 67.6 %reduce-scatter.36.cloned.1.call-done = f32[96,512]{1,0:T(8,128)} async-done(((f32[768,512]{1,0:T(8,128)}), f32[96,512]{1,0:T(8,128)}) %reduce-scatter.36.cloned.1.call-update) | async-done | bytes 196624 | tf_op jit(solution)/shard_map/reduce_scatter | solution.py:280
  673.0 68.0 %reduce-scatter.38.cloned.1.call-done = f32[512,96]{0,1:T(8,128)} async-done(((f32[512,768]{0,1:T(8,128)}), f32[512,96]{0,1:T(8,128)}) %reduce-scatter.38.cloned.1.call-update) | async-done | bytes 196624 | tf_op jit(solution)/shard_map/reduce_scatter | solution.py:281
  741.0 69.7 %reduce-scatter.32.cloned.1.call-done = f32[96,576]{1,0:T(8,128)} async-done(((f32[768,576]{1,0:T(8,128)}), f32[96,576]{1,0:T(8,128)}) %reduce-scatter.32.cloned.1.call-update) | async-done | bytes 221200 | tf_op jit(solution)/shard_map/reduce_scatter | solution.py:277
  (321 shorter events, 124.5 us)
Async XLA Ops:
  7.2 88.3 %copy-start = (bf16[768,576]{0,1:T(8,128)(2,1)S(1)}, bf16[768,576]{0,1:T(8,128)(2,1)}, u32[]{:S(2)}) copy-start(bf16[768,576]{0,1:T(8,128)(2,1)} %param.27) | copy-start | bytes 2654212
  9.1 32.9 %copy-start.29 = (bf16[2048,192]{0,1:T(8,128)(2,1)S(1)}, bf16[2048,192]{0,1:T(8,128)(2,1)}, u32[]{:S(2)}) copy-start(bf16[2048,192]{0,1:T(8,128)(2,1)} %param.23) | copy-start | bytes 2359300
  34.7 13.7 %all-to-all-start = ((s32[8,1,128]{2,1,0:T(1,128)}), s32[8,1,128]{2,1,0:T(1,128)S(1)}, u32[]{:S(2)}, u32[]{:S(2)}) async-start(s32[8,1,128]{2,1,0:T(1,128)} %reshape.467), calls=%async_computation | async-start | bytes 8192 | tf_op jit(solution)/shard_map/all_to_all | solution.py:100
  55.2 16.9 %all-to-all-start.1 = ((bf16[2,8,64,192]{3,2,0,1:T(8,128)(2,1)}), bf16[2,8,64,192]{3,2,0,1:T(8,128)(2,1)S(1)}, u32[]{:S(2)}, u32[]{:S(2)}) async-start(bf16[2,8,64,192]{3,2,0,1:T(8,128)(2,1)} %pad_maximum_fusion.1), calls=%async_computation.1 | async-start | bytes 1048576 | tf_op jit(solution)/shard_map/all_to_all | solution.py:103
  58.9 36.6 %all-gather.4.cloned.1.call-start = ((), (), s32[]{:S(2)}) async-start(), calls=%async_computation.16 | async-start | bytes 1966080 | tf_op jit(solution)/shard_map/all_gather | solution.py:110
  76.5 70.1 %reduce-scatter.18.cloned.1.call-start = ((), (), s32[]{:S(2)}) async-start(), calls=%async_computation.17 | async-start | bytes 1966080 | tf_op jit(solution)/shard_map/reduce_scatter | solution.py:148
  115.5 32.9 %copy-start.42 = (f32[768]{0:T(1024)S(1)}, f32[768]{0:T(1024)}, u32[]{:S(2)}) copy-start(f32[768]{0:T(1024)} %param.29) | copy-start | bytes 9220
  118.3 51.8 %all-gather.6.cloned.1.call-start = ((), (), s32[]{:S(2)}) async-start(), calls=%async_computation.18 | async-start | bytes 1966080 | tf_op jit(solution)/shard_map/all_gather | solution.py:156
  150.3 59.2 %reduce-scatter.22.cloned.1.call-start = ((), (), s32[]{:S(2)}) async-start(), calls=%async_computation.20 | async-start | bytes 1966080 | tf_op jit(solution)/shard_map/reduce_scatter | solution.py:180
  181.2 52.3 %all-gather.8.cloned.1.call-start = ((), (), s32[]{:S(2)}) async-start(), calls=%async_computation.21 | async-start | bytes 1966080 | tf_op jit(solution)/shard_map/all_gather | solution.py:193
  181.3 52.2 %copy-start.39 = (bf16[192,768]{1,0:T(8,128)(2,1)S(1)}, bf16[192,768]{1,0:T(8,128)(2,1)}, u32[]{:S(2)}) copy-start(bf16[192,768]{1,0:T(8,128)(2,1)} %param.28) | copy-start | bytes 884740
  213.6 81.1 %reduce-scatter.24.cloned.1.call-start = ((), (), s32[]{:S(2)}) async-start(), calls=%async_computation.22 | async-start | bytes 1966080 | tf_op jit(solution)/shard_map/reduce_scatter | solution.py:245
  266.4 59.2 %reduce-scatter.20.cloned.1.call-start = ((), (), s32[]{:S(2)}) async-start(), calls=%async_computation.19 | async-start | bytes 1966080 | tf_op jit(solution)/shard_map/reduce_scatter | solution.py:162
  268.7 57.0 %copy-start.8 = (bf16[256,768]{1,0:T(8,128)(2,1)S(1)}, bf16[256,768]{1,0:T(8,128)(2,1)}, u32[]{:S(2)}) copy-start(bf16[256,768]{1,0:T(8,128)(2,1)} %reduce-scatter.18.cloned.1.call-done) | copy-start | bytes 1179652
  268.7 57.0 %copy-start.10 = (bf16[256,768]{1,0:T(8,128)(2,1)S(1)}, bf16[256,768]{1,0:T(8,128)(2,1)}, u32[]{:S(2)}) copy-start(bf16[256,768]{1,0:T(8,128)(2,1)} %reduce-scatter.22.cloned.1.call-done) | copy-start | bytes 1179652
  268.7 57.0 %copy-start.44 = (f32[768]{0:T(1024)S(1)}, f32[768]{0:T(1024)}, u32[]{:S(2)}) copy-start(f32[768]{0:T(1024)} %param.29) | copy-start | bytes 9220
  268.7 57.0 %copy-start.49 = (f32[256]{0:T(256)S(1)}, f32[256]{0:T(256)}, u32[]{:S(2)}) copy-start(f32[256]{0:T(256)} %copy-done.47) | copy-start | bytes 3076
  268.7 57.0 %copy-start.54 = (f32[256]{0:T(256)S(1)}, f32[256]{0:T(256)}, u32[]{:S(2)}) copy-start(f32[256]{0:T(256)} %get-tuple-element.358) | copy-start | bytes 3076
  268.7 57.0 %copy-start.56 = (f32[256]{0:T(256)S(1)}, f32[256]{0:T(256)}, u32[]{:S(2)}) copy-start(f32[256]{0:T(256)} %copy-done.55) | copy-start | bytes 3076
  268.7 57.0 %copy-start.57 = (f32[256]{0:T(256)S(1)}, f32[256]{0:T(256)}, u32[]{:S(2)}) copy-start(f32[256]{0:T(256)} %get-tuple-element.356) | copy-start | bytes 3076
  268.7 127.1 %reduce-scatter.30.cloned.1.call-start = ((), (), s32[]{:S(2)}) async-start(), calls=%async_computation.25 | async-start | bytes 1327104 | tf_op jit(solution)/shard_map/reduce_scatter | solution.py:282
  296.0 32.2 %copy-start.23 = (bf16[256,192]{1,0:T(8,128)(2,1)S(1)}, bf16[256,192]{1,0:T(8,128)(2,1)}, u32[]{:S(2)}) copy-start(bf16[256,192]{1,0:T(8,128)(2,1)} %copy-done.22) | copy-start | bytes 294916
  329.7 130.8 %reduce-scatter.40.cloned.1.call-start = ((), (), s32[]{:S(2)}) async-start(), calls=%async_computation.30 | async-start | bytes 884736
  360.8 20.0 %all-to-all-start.2 = ((bf16[2,8,64,192]{3,2,0,1:T(8,128)(2,1)}), bf16[2,8,64,192]{3,2,0,1:T(8,128)(2,1)S(1)}, u32[]{:S(2)}, u32[]{:S(2)}) async-start(bf16[2,8,64,192]{3,2,0,1:T(8,128)(2,1)} %copy.69), calls=%async_computation.6 | async-start | bytes 1048576 | tf_op jit(solution)/shard_map/all_to_all | solution.py:262
  366.3 122.5 %reduce-scatter.26.cloned.1.call-start = ((), (), s32[]{:S(2)}) async-start(), calls=%async_computation.23 | async-start | bytes 1310720 | tf_op jit(solution)/shard_map/reduce_scatter | solution.py:287
  387.4 127.2 %reduce-scatter.28.cloned.1.call-start = ((), (), s32[]{:S(2)}) async-start(), calls=%async_computation.24 | async-start | bytes 1310720 | tf_op jit(solution)/shard_map/reduce_scatter | solution.py:290
  392.7 143.4 %reduce-scatter.42.cloned.1.call-start = ((), (), s32[]{:S(2)}) async-start(), calls=%async_computation.31 | async-start | bytes 92160
  397.4 208.0 %reduce-scatter.34.cloned.1.call-start = ((), (), s32[]{:S(2)}) async-start(), calls=%async_computation.27 | async-start | bytes 1769472 | tf_op jit(solution)/shard_map/reduce_scatter | solution.py:279
  401.6 271.4 %reduce-scatter.36.cloned.1.call-start = ((), (), s32[]{:S(2)}) async-start(), calls=%async_computation.28 | async-start | bytes 1769472 | tf_op jit(solution)/shard_map/reduce_scatter | solution.py:280
  403.9 337.2 %reduce-scatter.38.cloned.1.call-start = ((), (), s32[]{:S(2)}) async-start(), calls=%async_computation.29 | async-start | bytes 1769472 | tf_op jit(solution)/shard_map/reduce_scatter | solution.py:281
  408.3 402.5 %reduce-scatter.32.cloned.1.call-start = ((), (), s32[]{:S(2)}) async-start(), calls=%async_computation.26 | async-start | bytes 2211840 | tf_op jit(solution)/shard_map/reduce_scatter | solution.py:277
  412.5 49.7 %copy-start.50 = (f32[768]{0:T(1024)S(1)}, f32[768]{0:T(1024)}, u32[]{:S(2)}) copy-start(f32[768]{0:T(1024)} %get-tuple-element.277) | copy-start | bytes 9220
  (58 other events, 516.1 us)
Sparse Core Ops, SparseCore 0:
  76.6 18.7 all-gather.3
  118.4 28.1 reduce-scatter.17
  150.5 19.6 all-gather.5
  181.3 28.1 reduce-scatter.21
  213.8 19.6 all-gather.7
  266.6 28.1 reduce-scatter.23
  297.4 28.1 reduce-scatter.19
  329.8 65.9 reduce-scatter.29
  399.1 61.3 reduce-scatter.39
  463.1 23.8 reduce-scatter.25
  489.6 25.0 reduce-scatter.27
  517.0 19.0 reduce-scatter.41
  540.5 64.8 reduce-scatter.33
  609.2 63.7 reduce-scatter.35
  677.2 63.7 reduce-scatter.37
  745.0 65.7 reduce-scatter.31
where the time goes:
time: 823 us; the launch traced here: 818 us
  waiting for transfers between devices  567 us (69%)
  local copies, waits for them, and re-layouts  78 us (9%)
  matrix products  64.8 us (8%)
  other arithmetic  45 us (5%)
  blocking collectives  25.2 us (3%)
  starting transfers between devices  18.2 us (2%)
  between operations  16.5 us (2%)
    reduce_scatter x1, waiting for transfers between devices, shards(): lax.psum_scatter(attend_grad, 'dp', scatter_dimension=0, tiled=True)  69.7 us
    reduce_scatter x1, waiting for transfers between devices, shards(): lax.psum_scatter(down_grad, 'dp', scatter_dimension=1, tiled=True)  68 us
    reduce_scatter x1, waiting for transfers between devices, shards(): lax.psum_scatter(gate_grad, 'dp', scatter_dimension=0, tiled=True)  67.9 us
    reduce_scatter x1, waiting for transfers between devices, shards(): lax.psum_scatter(up_grad, 'dp', scatter_dimension=0, tiled=True)  67.6 us
    unnamed x18, waiting for transfers between devices  65.6 us
    reduce_scatter x1, waiting for transfers between devices, shards(): lax.psum_scatter(jnp.dot(part_rows, down_weight, preferred_element_type=j...  29.6 us
    reduce_scatter x1, waiting for transfers between devices, shards(): lax.psum_scatter((jnp.dot(gate_back, gate_weight.T, preferred_element_typ...  28.3 us
    reduce_scatter x1, waiting for transfers between devices, shards(): lax.psum_scatter(jnp.dot(part_rows, output_weight, preferred_element_type...  28.3 us
  transfers between devices with their start and end apart: 19, of which 18 were waited for; matrix products, arithmetic and copies ran while one was open for 9% of the time, Pallas kernels for 0%

commit v1 on v0

--- a/solution.py
+++ b/solution.py
@@ -153,7 +153,25 @@
     ).astype(jnp.float32)
     after = inputs + branch_one
     normed_two, second_scale = normed_rows(after, second_gain)
-    normed_two_full = lax.all_gather(normed_two.astype(jnp.bfloat16), "tensor", axis=0, tiled=True)
+    shard = normed_two.astype(jnp.bfloat16)
+    peers, position_2, rows = (lax.axis_size("tensor"), lax.axis_index("tensor"), shard.shape[0])
+    upward = [(i, (i + 1) % peers) for i in range(peers)]
+    backward = [(i, (i - 1) % peers) for i in range(peers)]
+    result_2 = jnp.zeros((*shard.shape[:0], peers * rows, *shard.shape[0 + 1 :]), shard.dtype)
+    result_2 = lax.dynamic_update_slice_in_dim(result_2, shard, position_2 * rows, axis=0)
+    from_left = from_right = shard
+    middle = peers // 2
+    for step in range(1, middle + 1):
+        from_left = lax.ppermute(from_left, "tensor", upward)
+        result_2 = lax.dynamic_update_slice_in_dim(
+            result_2, from_left, (position_2 - step) % peers * rows, axis=0
+        )
+        if step < peers - middle:
+            from_right = lax.ppermute(from_right, "tensor", backward)
+            result_2 = lax.dynamic_update_slice_in_dim(
+                result_2, from_right, (position_2 + step) % peers * rows, axis=0
+            )
+    normed_two_full = result_2
     gate = jnp.dot(normed_two_full, gate_weight, preferred_element_type=jnp.float32)
     up_part = jnp.dot(normed_two_full, up_weight, preferred_element_type=jnp.float32)
     sigmoid_gate = jax.nn.sigmoid(gate)

time: 823 us -> 823 us (level)
  waiting for transfers between devices: 567 us -> 554 us
    all_gather x1 -> x0, waiting for transfers between devices: 19.8 us -> none  [shards(): lax.all_gather(normed_two.astype(jnp.bfloat16), 'tensor', axis=0, tiled=T...]
    ppermute x0 -> x3, waiting for transfers between devices: none -> 11.7 us  [the longest x2 11.7 us: shards(): from_left = lax.ppermute(from_left, 'tensor', upward)]
    unnamed x18 -> x17, waiting for transfers between devices: 65.6 us -> 64.4 us
  transfers between devices with their start and end apart: 19 -> 21, of which waited for: 18 -> 18; matrix products, arithmetic and copies ran while one was open for 9% -> 10% of each run, Pallas kernels for 0% -> 0%
where the time goes in v1:
time: 823 us; the launch traced here: 817 us
  waiting for transfers between devices  554 us (67%)
  local copies, waits for them, and re-layouts  81.6 us (10%)
  matrix products  68.2 us (8%)
  other arithmetic  48.8 us (6%)
  blocking collectives  25.3 us (3%)
  starting transfers between devices  19.9 us (2%)
  between operations  16.5 us (2%)
    reduce_scatter x1, waiting for transfers between devices, shards(): lax.psum_scatter(attend_grad, 'dp', scatter_dimension=0, tiled=True)  69.6 us
    reduce_scatter x1, waiting for transfers between devices, shards(): lax.psum_scatter(down_grad, 'dp', scatter_dimension=1, tiled=True)  68 us
    reduce_scatter x1, waiting for transfers between devices, shards(): lax.psum_scatter(up_grad, 'dp', scatter_dimension=0, tiled=True)  67.8 us
    reduce_scatter x1, waiting for transfers between devices, shards(): lax.psum_scatter(gate_grad, 'dp', scatter_dimension=0, tiled=True)  67.8 us
    unnamed x17, waiting for transfers between devices  64.4 us
    reduce_scatter x1, waiting for transfers between devices, shards(): lax.psum_scatter(jnp.dot(part_rows, down_weight, preferred_element_type=j...  29.5 us
    reduce_scatter x1, waiting for transfers between devices, shards(): lax.psum_scatter(jnp.dot(part_rows, output_weight, preferred_element_type...  28.3 us
    reduce_scatter x1, waiting for transfers between devices, shards(): lax.psum_scatter((jnp.dot(gate_back, gate_weight.T, preferred_element_typ...  27.9 us
  transfers between devices with their start and end apart: 21, of which 18 were waited for; matrix products, arithmetic and copies ran while one was open for 10% of the time, Pallas kernels for 0%

profile of v1, /device:TPU:0, one launch (start us, length us, event | category | flops | bytes accessed | tf_op | source)
XLA Modules:
  0.0 817.3 jit_solution(16036438366193117796)
XLA Ops:
  9.2 12.4 %scatter_fusion = s32[2,512]{1,0:T(2,128)S(1)} fusion(s32[2,512]{1,0:T(2,128)S(1)} %broadcast_in_dim.53, s32[256]{0:T(256)S(1)} %bitcast.157, s32[256]{0:T(256)S(1)} %get-tuple-element.364), kind=kCustom, calls=%fused_computation.4 | custom fusion | bytes 5120 | tf_op jit(solution)/shard_map/scatter | solution.py:97
  21.6 12.4 %scatter_fusion.1 = s32[2,512]{1,0:T(2,128)S(1)} fusion(s32[2,512]{1,0:T(2,128)S(1)} %scatter_fusion, s32[256]{0:T(256)S(1)} %bitcast.159, s32[256]{0:T(256)S(1)} %get-tuple-element.362), kind=kCustom, calls=%fused_computation.5 | custom fusion | bytes 5120 | tf_op jit(solution)/shard_map/scatter | solution.py:98
  34.7 7.3 all-to-all-start
  44.0 4.4 all-to-all-done
  58.8 13.2 %all-to-all-done.1 = bf16[2,8,64,192]{3,2,0,1:T(8,128)(2,1)S(1)} async-done(((bf16[2,8,64,192]{3,2,0,1:T(8,128)(2,1)}), bf16[2,8,64,192]{3,2,0,1:T(8,128)(2,1)S(1)}, u32[]{:S(2)}, u32[]{:S(2)}) %all-to-all-start.1) | async-done | bytes 393248 | tf_op jit(solution)/shard_map/all_to_all | solution.py:103
  77.5 17.7 %all-gather.3.cloned.1.call-done = bf16[1024,768]{1,0:T(8,128)(2,1)} async-done(((bf16[256,768]{1,0:T(8,128)(2,1)}), bf16[1024,768]{1,0:T(8,128)(2,1)}) %all-gather.3.cloned.1.call-update) | async-done | bytes 1572880 | tf_op jit(solution)/shard_map/all_gather | solution.py:110
  98.5 15.5 %while.30 = (s32[]{:T(128)}, bf16[2,512,3,64]{1,3,2,0:T(8,128)(2,1)S(1)}, f32[2,3,512]{2,1,0:T(4,128)S(1)}, s32[2]{0:T(128)S(1)}, s32[]{:T(128)}, /*index=5*/bf1...) while((s32[]{:T(128)}, ...), condition=%wide.region_8.9_spmd.clone.clone, body=%wide.region_5.8_spmd.clone.clone.sunk | while | flops 422674432 | bytes 22216908 | solution.py:145
  118.1 28.3 %reduce-scatter.18.cloned.1.call-done = bf16[256,768]{1,0:T(8,128)(2,1)} async-done(((bf16[1024,768]{1,0:T(8,128)(2,1)}), bf16[256,768]{1,0:T(8,128)(2,1)}) %reduce-scatter.18.cloned.1.call-update) | async-done | bytes 393232 | tf_op jit(solution)/shard_map/reduce_scatter | solution.py:148
  152.3 9.3 %collective-permute-done = bf16[256,768]{1,0:T(8,128)(2,1)S(1)} collective-permute-done((bf16[256,768]{1,0:T(8,128)(2,1)}, bf16[256,768]{1,0:T(8,128)(2,1)S(1)}, u32[]{:S(2)}, u32[]{:S(2)}) %collective-permute-start) | collective-permute-done | bytes 393248 | tf_op jit(solution)/shard_map/ppermute | solution.py:165
  173.2 4.3 multiply_convert_fusion.1
  181.4 27.9 %reduce-scatter.22.cloned.1.call-done = bf16[256,768]{1,0:T(8,128)(2,1)} async-done(((bf16[1024,768]{1,0:T(8,128)(2,1)}), bf16[256,768]{1,0:T(8,128)(2,1)}) %reduce-scatter.22.cloned.1.call-update) | async-done | bytes 393232 | tf_op jit(solution)/shard_map/reduce_scatter | solution.py:198
  213.4 19.7 %all-gather.5.cloned.1.call-done = bf16[1024,768]{1,0:T(8,128)(2,1)} async-done(((bf16[256,768]{1,0:T(8,128)(2,1)}), bf16[1024,768]{1,0:T(8,128)(2,1)}) %all-gather.5.cloned.1.call-update) | async-done | bytes 1572880 | tf_op jit(solution)/shard_map/all_gather | solution.py:211
  235.9 23.7 %while.31 = (s32[]{:T(128)}, f32[1024,3,64]{0,2,1:T(8,128)S(1)}, f32[1024,3,64]{0,2,1:T(8,128)}, bf16[2,512,3,64]{1,3,2,0:T(8,128)(2,1)}, s32[2]{0:T(128)S(1)}, ...) while((s32[]{:T(128)}, f32[1024,3,64]{0,2,1:T(8,128)S(1)}, ...), condition=%wide.region_16.17_spmd.clone.clone, body=%wide.region_14.16_spmd.clone.clone.sunk | while | flops 1032355840 | bytes 67424672 | solution.py:250
  268.7 25.8 %reduce-scatter.24.cloned.1.call-done = bf16[256,768]{1,0:T(8,128)(2,1)} async-done(((bf16[1024,768]{1,0:T(8,128)(2,1)}), bf16[256,768]{1,0:T(8,128)(2,1)}) %reduce-scatter.24.cloned.1.call-update) | async-done | bytes 393232 | tf_op jit(solution)/shard_map/reduce_scatter | solution.py:263
  295.7 29.5 %reduce-scatter.20.cloned.1.call-done = bf16[256,768]{1,0:T(8,128)(2,1)} async-done(((bf16[1024,768]{1,0:T(8,128)(2,1)}), bf16[256,768]{1,0:T(8,128)(2,1)}) %reduce-scatter.20.cloned.1.call-update) | async-done | bytes 393232 | tf_op jit(solution)/shard_map/reduce_scatter | solution.py:180
  333.2 13.1 %scatter_fusion.2 = f32[2,512,192]{2,1,0:T(8,128)S(1)} fusion(f32[2,512,192]{2,1,0:T(8,128)S(1)} %broadcast_in_dim.61, s32[256]{0:T(256)S(1)} %bitcast.158, f32[256,192]{1,0:T(8,128)S(1)} %get-tuple-element.349), kind=kCustom, calls=%fused_computation.6 | custom fusion | bytes 591872 | tf_op jit(solution)/shard_map/scatter | solution.py:277
  346.3 13.1 %scatter_fusion.3 = f32[2,512,192]{2,1,0:T(8,128)S(1)} fusion(f32[2,512,192]{2,1,0:T(8,128)S(1)} %scatter_fusion.2, s32[256]{0:T(256)S(1)} %bitcast.160, f32[256,192]{1,0:T(8,128)S(1)} %get-tuple-element.348), kind=kCustom, calls=%fused_computation.7 | custom fusion | bytes 591872 | tf_op jit(solution)/shard_map/scatter | solution.py:278
  360.4 5.5 all-to-all-start.2
  366.1 14.3 %all-to-all-done.2 = bf16[2,8,64,192]{3,2,0,1:T(8,128)(2,1)S(1)} async-done(((bf16[2,8,64,192]{3,2,0,1:T(8,128)(2,1)}), bf16[2,8,64,192]{3,2,0,1:T(8,128)(2,1)S(1)}, u32[]{:S(2)}, u32[]{:S(2)}) %all-to-all-start.2) | async-done | bytes 393248 | tf_op jit(solution)/shard_map/all_to_all | solution.py:280
  380.5 5.0 scatter_custom_fusion.4
  388.2 5.0 scatter_custom_fusion.5
  397.7 3.7 fusion.89
  409.3 4.1 fusion.88
  415.9 44.3 %reduce-scatter.40.cloned.1.call-done = f32[96,192]{1,0:T(8,128)} async-done(((f32[768,192]{1,0:T(8,128)}), f32[96,192]{1,0:T(8,128)}) %reduce-scatter.40.cloned.1.call-update) | async-done | bytes 73744
  461.9 19.6 %all-reduce.7 = (bf16[768]{0:T(1024)(128)(2,1)S(1)}, bf16[768]{0:T(1024)(128)(2,1)S(1)}) all-reduce(f32[768]{0:T(1024)S(1)} %get-tuple-element.279, f32[768]{0:T(1024)S(1)} %copy-done.51), channel_id=10, replica_groups=mesh['dp'=8,'tensor'=4] {'dp'}, use_global_device_ids=true, to_apply=%region_28.29.clone | all-reduce | flops 1536 | bytes 9216
  481.6 5.7 all-reduce.8
  490.4 23.9 %reduce-scatter.28.cloned.1.call-done = bf16[512,192]{1,0:T(8,128)(2,1)} async-done(((bf16[2048,192]{1,0:T(8,128)(2,1)}), bf16[512,192]{1,0:T(8,128)(2,1)}) %reduce-scatter.28.cloned.1.call-update) | async-done | bytes 196624 | tf_op jit(solution)/shard_map/reduce_scatter | solution.py:308
  516.1 19.8 %reduce-scatter.42.cloned.1.call-done = bf16[384,24]{0,1:T(8,128)(2,1)} async-done(((bf16[384,96]{0,1:T(8,128)(2,1)}), bf16[384,24]{0,1:T(8,128)(2,1)}) %reduce-scatter.42.cloned.1.call-update) | async-done | bytes 18448
  537.3 67.8 %reduce-scatter.34.cloned.1.call-done = f32[96,512]{1,0:T(8,128)} async-done(((f32[768,512]{1,0:T(8,128)}), f32[96,512]{1,0:T(8,128)}) %reduce-scatter.34.cloned.1.call-update) | async-done | bytes 196624 | tf_op jit(solution)/shard_map/reduce_scatter | solution.py:297
  605.0 67.8 %reduce-scatter.36.cloned.1.call-done = f32[96,512]{1,0:T(8,128)} async-done(((f32[768,512]{1,0:T(8,128)}), f32[96,512]{1,0:T(8,128)}) %reduce-scatter.36.cloned.1.call-update) | async-done | bytes 196624 | tf_op jit(solution)/shard_map/reduce_scatter | solution.py:298
  672.9 68.0 %reduce-scatter.38.cloned.1.call-done = f32[512,96]{0,1:T(8,128)} async-done(((f32[512,768]{0,1:T(8,128)}), f32[512,96]{0,1:T(8,128)}) %reduce-scatter.38.cloned.1.call-update) | async-done | bytes 196624 | tf_op jit(solution)/shard_map/reduce_scatter | solution.py:299
  740.9 69.6 %reduce-scatter.32.cloned.1.call-done = f32[96,576]{1,0:T(8,128)} async-done(((f32[768,576]{1,0:T(8,128)}), f32[96,576]{1,0:T(8,128)}) %reduce-scatter.32.cloned.1.call-update) | async-done | bytes 221200 | tf_op jit(solution)/shard_map/reduce_scatter | solution.py:295
  (329 shorter events, 135.2 us)
Async XLA Ops:
  7.2 88.1 %copy-start = (bf16[768,576]{0,1:T(8,128)(2,1)S(1)}, bf16[768,576]{0,1:T(8,128)(2,1)}, u32[]{:S(2)}) copy-start(bf16[768,576]{0,1:T(8,128)(2,1)} %param.27) | copy-start | bytes 2654212
  9.1 32.9 %copy-start.30 = (bf16[2048,192]{0,1:T(8,128)(2,1)S(1)}, bf16[2048,192]{0,1:T(8,128)(2,1)}, u32[]{:S(2)}) copy-start(bf16[2048,192]{0,1:T(8,128)(2,1)} %param.23) | copy-start | bytes 2359300
  34.7 13.7 %all-to-all-start = ((s32[8,1,128]{2,1,0:T(1,128)}), s32[8,1,128]{2,1,0:T(1,128)S(1)}, u32[]{:S(2)}, u32[]{:S(2)}) async-start(s32[8,1,128]{2,1,0:T(1,128)} %reshape.467), calls=%async_computation | async-start | bytes 8192 | tf_op jit(solution)/shard_map/all_to_all | solution.py:100
  55.1 16.9 %all-to-all-start.1 = ((bf16[2,8,64,192]{3,2,0,1:T(8,128)(2,1)}), bf16[2,8,64,192]{3,2,0,1:T(8,128)(2,1)S(1)}, u32[]{:S(2)}, u32[]{:S(2)}) async-start(bf16[2,8,64,192]{3,2,0,1:T(8,128)(2,1)} %pad_maximum_fusion.1), calls=%async_computation.1 | async-start | bytes 1048576 | tf_op jit(solution)/shard_map/all_to_all | solution.py:103
  58.7 36.6 %all-gather.3.cloned.1.call-start = ((), (), s32[]{:S(2)}) async-start(), calls=%async_computation.16 | async-start | bytes 1966080 | tf_op jit(solution)/shard_map/all_gather | solution.py:110
  76.3 70.0 %reduce-scatter.18.cloned.1.call-start = ((), (), s32[]{:S(2)}) async-start(), calls=%async_computation.17 | async-start | bytes 1966080 | tf_op jit(solution)/shard_map/reduce_scatter | solution.py:148
  118.0 91.2 %reduce-scatter.22.cloned.1.call-start = ((), (), s32[]{:S(2)}) async-start(), calls=%async_computation.19 | async-start | bytes 1966080 | tf_op jit(solution)/shard_map/reduce_scatter | solution.py:198
  150.5 11.1 %collective-permute-start = (bf16[256,768]{1,0:T(8,128)(2,1)}, bf16[256,768]{1,0:T(8,128)(2,1)S(1)}, u32[]{:S(2)}, u32[]{:S(2)}) collective-permute-start(bf16[256,768]{1,0:T(8,128)(2,1)} %get-tuple-element.324), channel_id=1, source_target_pairs={{0,1},{1,2},{2,3},{3,0},{4,5},{5,6},{6,7},{7,4},{8,9},{9,10},{10,1... | collective-permute-start | bytes 1179656 | tf_op jit(solution)/shard_map/ppermute | solution.py:165
  150.5 14.2 %collective-permute-start.1 = (bf16[256,768]{1,0:T(8,128)(2,1)}, bf16[256,768]{1,0:T(8,128)(2,1)}, u32[]{:S(2)}, u32[]{:S(2)}) collective-permute-start(bf16[256,768]{1,0:T(8,128)(2,1)} %get-tuple-element.324), channel_id=1, source_target_pairs={{0,3},{1,0},{2,1},{3,2},{4,7},{5,4},{6,5},{7,6},{8,11},{9,8},{10,9... | collective-permute-start | bytes 1179656 | tf_op jit(solution)/shard_map/ppermute | solution.py:170
  161.6 7.3 collective-permute-start.2
  181.1 52.0 %copy-start.40 = (bf16[192,768]{1,0:T(8,128)(2,1)S(1)}, bf16[192,768]{1,0:T(8,128)(2,1)}, u32[]{:S(2)}) copy-start(bf16[192,768]{1,0:T(8,128)(2,1)} %param.28) | copy-start | bytes 884740
  181.1 52.0 %all-gather.5.cloned.1.call-start = ((), (), s32[]{:S(2)}) async-start(), calls=%async_computation.20 | async-start | bytes 1966080 | tf_op jit(solution)/shard_map/all_gather | solution.py:211
  213.3 81.1 %reduce-scatter.24.cloned.1.call-start = ((), (), s32[]{:S(2)}) async-start(), calls=%async_computation.21 | async-start | bytes 1966080 | tf_op jit(solution)/shard_map/reduce_scatter | solution.py:263
  266.1 59.1 %reduce-scatter.20.cloned.1.call-start = ((), (), s32[]{:S(2)}) async-start(), calls=%async_computation.18 | async-start | bytes 1966080 | tf_op jit(solution)/shard_map/reduce_scatter | solution.py:180
  268.3 56.8 %copy-start.8 = (bf16[256,768]{1,0:T(8,128)(2,1)S(1)}, bf16[256,768]{1,0:T(8,128)(2,1)}, u32[]{:S(2)}) copy-start(bf16[256,768]{1,0:T(8,128)(2,1)} %reduce-scatter.18.cloned.1.call-done) | copy-start | bytes 1179652
  268.3 56.8 %copy-start.10 = (bf16[256,768]{1,0:T(8,128)(2,1)S(1)}, bf16[256,768]{1,0:T(8,128)(2,1)}, u32[]{:S(2)}) copy-start(bf16[256,768]{1,0:T(8,128)(2,1)} %reduce-scatter.22.cloned.1.call-done) | copy-start | bytes 1179652
  268.3 56.8 %copy-start.45 = (f32[768]{0:T(1024)S(1)}, f32[768]{0:T(1024)}, u32[]{:S(2)}) copy-start(f32[768]{0:T(1024)} %param.29) | copy-start | bytes 9220
  268.3 56.8 %copy-start.50 = (f32[256]{0:T(256)S(1)}, f32[256]{0:T(256)}, u32[]{:S(2)}) copy-start(f32[256]{0:T(256)} %copy-done.48) | copy-start | bytes 3076
  268.3 56.8 %copy-start.55 = (f32[256]{0:T(256)S(1)}, f32[256]{0:T(256)}, u32[]{:S(2)}) copy-start(f32[256]{0:T(256)} %get-tuple-element.360) | copy-start | bytes 3076
  268.4 56.8 %copy-start.57 = (f32[256]{0:T(256)S(1)}, f32[256]{0:T(256)}, u32[]{:S(2)}) copy-start(f32[256]{0:T(256)} %copy-done.56) | copy-start | bytes 3076
  268.4 56.8 %copy-start.58 = (f32[256]{0:T(256)S(1)}, f32[256]{0:T(256)}, u32[]{:S(2)}) copy-start(f32[256]{0:T(256)} %get-tuple-element.358) | copy-start | bytes 3076
  268.4 127.7 %reduce-scatter.30.cloned.1.call-start = ((), (), s32[]{:S(2)}) async-start(), calls=%async_computation.24 | async-start | bytes 1327104 | tf_op jit(solution)/shard_map/reduce_scatter | solution.py:300
  329.3 131.0 %reduce-scatter.40.cloned.1.call-start = ((), (), s32[]{:S(2)}) async-start(), calls=%async_computation.29 | async-start | bytes 884736
  360.4 20.0 %all-to-all-start.2 = ((bf16[2,8,64,192]{3,2,0,1:T(8,128)(2,1)}), bf16[2,8,64,192]{3,2,0,1:T(8,128)(2,1)S(1)}, u32[]{:S(2)}, u32[]{:S(2)}) async-start(bf16[2,8,64,192]{3,2,0,1:T(8,128)(2,1)} %copy.69), calls=%async_computation.6 | async-start | bytes 1048576 | tf_op jit(solution)/shard_map/all_to_all | solution.py:280
  365.9 122.7 %reduce-scatter.26.cloned.1.call-start = ((), (), s32[]{:S(2)}) async-start(), calls=%async_computation.22 | async-start | bytes 1310720 | tf_op jit(solution)/shard_map/reduce_scatter | solution.py:305
  388.2 126.1 %reduce-scatter.28.cloned.1.call-start = ((), (), s32[]{:S(2)}) async-start(), calls=%async_computation.23 | async-start | bytes 1310720 | tf_op jit(solution)/shard_map/reduce_scatter | solution.py:308
  396.0 139.9 %reduce-scatter.42.cloned.1.call-start = ((), (), s32[]{:S(2)}) async-start(), calls=%async_computation.30 | async-start | bytes 92160
  397.7 207.4 %reduce-scatter.34.cloned.1.call-start = ((), (), s32[]{:S(2)}) async-start(), calls=%async_computation.26 | async-start | bytes 1769472 | tf_op jit(solution)/shard_map/reduce_scatter | solution.py:297
  401.5 271.4 %reduce-scatter.36.cloned.1.call-start = ((), (), s32[]{:S(2)}) async-start(), calls=%async_computation.27 | async-start | bytes 1769472 | tf_op jit(solution)/shard_map/reduce_scatter | solution.py:298
  405.3 335.6 %reduce-scatter.38.cloned.1.call-start = ((), (), s32[]{:S(2)}) async-start(), calls=%async_computation.28 | async-start | bytes 1769472 | tf_op jit(solution)/shard_map/reduce_scatter | solution.py:299
  409.2 401.3 %reduce-scatter.32.cloned.1.call-start = ((), (), s32[]{:S(2)}) async-start(), calls=%async_computation.25 | async-start | bytes 2211840 | tf_op jit(solution)/shard_map/reduce_scatter | solution.py:295
  413.4 48.5 %copy-start.51 = (f32[768]{0:T(1024)S(1)}, f32[768]{0:T(1024)}, u32[]{:S(2)}) copy-start(f32[768]{0:T(1024)} %get-tuple-element.277) | copy-start | bytes 9220
  (61 other events, 567.4 us)
Sparse Core Ops, SparseCore 0:
  76.5 18.7 all-gather.2
  118.2 28.1 reduce-scatter.17
  181.2 27.9 reduce-scatter.21
  213.4 19.6 all-gather.4
  266.2 28.1 reduce-scatter.23
  297.0 28.1 reduce-scatter.19
  329.4 65.9 reduce-scatter.29
  398.7 61.4 reduce-scatter.39
  463.0 23.8 reduce-scatter.25
  489.2 25.0 reduce-scatter.27
  516.9 19.0 reduce-scatter.41
  540.2 64.8 reduce-scatter.33
  609.0 63.8 reduce-scatter.35
  677.1 63.7 reduce-scatter.37
  744.8 65.6 reduce-scatter.31
